TPU v7x, 32 devices: a whole 2x2x4 slice. The times are simulated.
32 devices in a mesh: segment: 2 (over core), dp: 4 (over y, x), mp: 4 (over z).
Axes of the slice: x: 2, y: 2, z: 4, core: 2. Of those that a mesh axis runs over, the one named last changes fastest.
Arguments:
- token_ids: int32 [2, 256], replicated, may hold values from 0 to 32767
- table: bfloat16 [32768, 8192], P('dp', 'mp'), may hold values from -6 to 6
- w_up: bfloat16 [2, 8192, 32768], P('segment', 'mp', 'dp'), may hold values from -0.0625 to 0.0625
- w_down: bfloat16 [2, 32768, 8192], P('segment', 'dp', 'mp'), may hold values from -0.03125 to 0.03125
- cotangent: bfloat16 [2, 256, 8192], P(None, 'dp', 'mp'), may hold values from -6 to 6
Outputs:
- acts: bfloat16 [2, 2, 256, 8192], P('segment', None, 'dp', 'mp')
- grads: bfloat16 [2, 2, 256, 8192], P('segment', None, 'dp', 'mp')
All inputs are finite; a program needn't handle non-finite values.
Results may differ from a plain program's by a relative error of at most 0.018.
Values may be sent and summed in bfloat16 or wider, within the bound.
A program may use at most 192 MiB of HBM per device.

v0:
```python
from functools import partial
import jax
import jax.numpy as jnp
from jax import lax
from jax.sharding import PartitionSpec as P

root_coef = 0.7978845608028654


def from_behind(value, axis, steps):
    count = lax.axis_size(axis)
    leading, last = (max(0, -steps), min(count, count - steps))
    return lax.ppermute(value, axis, [(source, source + steps) for source in range(leading, last)])


def gelu_value(value):
    return 0.5 * value * (1.0 + jnp.tanh(root_coef * (value + 0.044715 * value * value * value)))


def gelu_slope(value):
    inner = jnp.tanh(root_coef * (value + 0.044715 * value * value * value))
    return 0.5 * (1.0 + inner) + 0.5 * value * (1.0 - inner * inner) * root_coef * (
        1.0 + 0.134145 * value * value
    )


def forward_activate(summed):
    return (gelu_value(summed).astype(jnp.bfloat16), summed)


def backward_activate(saved, summed):
    return ((gelu_slope(saved) * summed).astype(jnp.bfloat16), saved)


def lookup(token_row, table):
    table_rows = table.shape[0]
    offset = lax.axis_index("dp") * table_rows
    picked = token_row - offset
    inside = (picked >= 0) & (picked < table_rows)
    fetched = jnp.take(table, jnp.clip(picked, 0, table_rows - 1), axis=0)
    return lax.psum_scatter(
        jnp.where(inside[:, None], fetched.astype(jnp.float32), 0.0).astype(jnp.bfloat16),
        "dp",
        scatter_dimension=0,
        tiled=True,
    )


def layer_pass(inputs, first_weight, first_dim, second_weight, second_dim, activate):
    partial_sum = lax.dot_general(
        lax.all_gather(inputs, "dp", axis=0, tiled=True),
        first_weight,
        (((1,), (first_dim,)), ((), ())),
        preferred_element_type=jnp.float32,
    )
    summed = lax.psum(partial_sum.astype(jnp.bfloat16), "mp").astype(jnp.float32)
    active, kept = activate(summed)
    mixed = lax.psum_scatter(
        lax.dot_general(
            active,
            second_weight,
            (((1,), (second_dim,)), ((), ())),
            preferred_element_type=jnp.float32,
        ).astype(jnp.bfloat16),
        "dp",
        scatter_dimension=0,
        tiled=True,
    ).astype(jnp.float32)
    return ((inputs.astype(jnp.float32) + mixed).astype(jnp.bfloat16), kept)


def on_device(token_ids, table, w_up, w_down, cotangent):
    micro_count = cotangent.shape[0]
    up_local = w_up[0]
    down_local = w_down[0]
    is_first = lax.axis_index("segment") == 0
    received = jnp.zeros(cotangent.shape[1:], jnp.bfloat16)
    kept_list = []
    forward_outs = []
    for tick in range(micro_count + 1):
        if tick < micro_count:
            entering = lookup(token_ids[tick], table)
        else:
            entering = jnp.zeros_like(received)
        inputs = jnp.where(is_first, entering, received)
        leaving, kept = layer_pass(inputs, up_local, 0, down_local, 0, forward_activate)
        kept_list.append(kept)
        forward_outs.append(leaving)
        if tick < micro_count:
            received = from_behind(leaving, "segment", 1)
    returned = jnp.zeros_like(received)
    backward_outs = []
    for tick in range(micro_count + 1):
        if tick < micro_count:
            given = cotangent[micro_count - 1 - tick]
        else:
            given = jnp.zeros_like(received)
        upstream = jnp.where(is_first, returned, given)
        activate = partial(backward_activate, kept_list[micro_count - tick])
        gradient, unused = layer_pass(upstream, down_local, 1, up_local, 1, activate)
        backward_outs.append(gradient)
        if tick < micro_count:
            returned = from_behind(gradient, "segment", -1)
    acts = jnp.stack(
        [
            jnp.where(is_first, forward_outs[micro_pos], forward_outs[micro_pos + 1])
            for micro_pos in range(micro_count)
        ]
    )
    grads = jnp.stack(
        [
            jnp.where(
                is_first,
                backward_outs[micro_count - micro_pos],
                backward_outs[micro_count - 1 - micro_pos],
            )
            for micro_pos in range(micro_count)
        ]
    )
    return (acts[None], grads[None])


def solution(mesh):
    return jax.shard_map(
        on_device,
        mesh=mesh,
        in_specs=(
            P(),
            P("dp", "mp"),
            P("segment", "mp", "dp"),
            P("segment", "dp", "mp"),
            P(None, "dp", "mp"),
        ),
        out_specs=(P("segment", None, "dp", "mp"), P("segment", None, "dp", "mp")),
        check_vma=False,
    )
```

profile of v0, /device:TPU:0, one launch (start us, length us, event | category | flops | bytes accessed | tf_op | source)
XLA Modules:
  0.0 1510.9 jit_solution(5395322229420565547)
XLA Ops:
  8.8 10.1 gather_fusion
  19.0 1.3 select_convert_fusion.1
  20.3 31.3 %reduce-scatter.9.cloned.1.call-done = bf16[64,2048]{1,0:T(8,128)(2,1)} async-done(((bf16[256,2048]{1,0:T(8,128)(2,1)}), bf16[64,2048]{1,0:T(8,128)(2,1)}) %reduce-scatter.9.cloned.1.call-update) | async-done | bytes 262160 | tf_op jit(solution)/shard_map/reduce_scatter | solution.py:41
  51.7 1.7 broadcast_select_fusion.3
  53.4 27.2 %all-gather.8.cloned.1.call-done = bf16[256,2048]{1,0:T(8,128)(2,1)} async-done(((bf16[64,2048]{1,0:T(8,128)(2,1)}), bf16[256,2048]{1,0:T(8,128)(2,1)}) %all-gather.8.cloned.1.call-update) | async-done | bytes 1048592 | tf_op jit(solution)/shard_map/all_gather | solution.py:51
  80.6 16.7 %fusion.24 = bf16[256,8192]{1,0:T(8,128)(2,1)} fusion(bf16[256,2048]{1,0:T(8,128)(2,1)} %all-gather.8.cloned.1.call-done, bf16[1,2048,8192]{2,1,0:T(8,128)(2,1)} %param.9), kind=kOutput, calls=%fused_computation.47 | convolution fusion | flops 8592031744 | bytes 38797312 | tf_op jit(solution)/shard_map/dot_general | solution.py:50
  97.4 155.1 %all-reduce.7.cloned.1.call-done = bf16[256,8192]{1,0:T(8,128)(2,1)} async-done(((bf16[256,8192]{1,0:T(8,128)(2,1)}), bf16[256,8192]{1,0:T(8,128)(2,1)}) %all-reduce.7.cloned.1.call-update) | async-done | bytes 4194320 | tf_op jit(solution)/shard_map/psum | solution.py:56
  252.5 18.7 %fusion.123 = bf16[256,2048]{1,0:T(8,128)(2,1)} fusion(bf16[1,8192,2048]{2,1,0:T(8,128)(2,1)} %param.10, bf16[256,8192]{1,0:T(8,128)(2,1)} %all-reduce.7.cloned.1.call-done), kind=kOutput, calls=%fused_computation.116 | convolution fusion | flops 8611430400 | bytes 38797312 | tf_op jit(solution)/shard_map/dot_general | solution.py:59
  271.5 10.3 gather_fusion.1
  281.8 1.3 select_convert_fusion
  283.2 15.1 reduce-scatter.11.cloned.1.call-done
  299.4 1.6 collective-permute-start
  301.0 28.1 %reduce-scatter.13.cloned.1.call-done = bf16[64,2048]{1,0:T(8,128)(2,1)} async-done(((bf16[256,2048]{1,0:T(8,128)(2,1)}), bf16[64,2048]{1,0:T(8,128)(2,1)}) %reduce-scatter.13.cloned.1.call-update) | async-done | bytes 262160 | tf_op jit(solution)/shard_map/reduce_scatter | solution.py:41
  329.0 1.7 broadcast_select_fusion.2
  330.8 27.0 %all-gather.10.cloned.1.call-done = bf16[256,2048]{1,0:T(8,128)(2,1)} async-done(((bf16[64,2048]{1,0:T(8,128)(2,1)}), bf16[256,2048]{1,0:T(8,128)(2,1)}) %all-gather.10.cloned.1.call-update) | async-done | bytes 1048592 | tf_op jit(solution)/shard_map/all_gather | solution.py:51
  357.8 16.6 %fusion.27 = bf16[256,8192]{1,0:T(8,128)(2,1)} fusion(bf16[256,2048]{1,0:T(8,128)(2,1)} %all-gather.10.cloned.1.call-done, bf16[1,2048,8192]{2,1,0:T(8,128)(2,1)} %param.9), kind=kOutput, calls=%fused_computation.48 | convolution fusion | flops 8592031744 | bytes 38797312 | tf_op jit(solution)/shard_map/dot_general | solution.py:50
  374.6 155.1 %all-reduce.9.cloned.1.call-done = bf16[256,8192]{1,0:T(8,128)(2,1)} async-done(((bf16[256,8192]{1,0:T(8,128)(2,1)}), bf16[256,8192]{1,0:T(8,128)(2,1)}) %all-reduce.9.cloned.1.call-update) | async-done | bytes 4194320 | tf_op jit(solution)/shard_map/psum | solution.py:56
  529.6 18.7 %fusion.128 = bf16[256,2048]{1,0:T(8,128)(2,1)} fusion(bf16[1,8192,2048]{2,1,0:T(8,128)(2,1)} %param.10, bf16[256,8192]{1,0:T(8,128)(2,1)} %all-reduce.9.cloned.1.call-done), kind=kOutput, calls=%fused_computation.117 | convolution fusion | flops 8611430400 | bytes 38797312 | tf_op jit(solution)/shard_map/dot_general | solution.py:59
  549.3 26.2 %reduce-scatter.15.cloned.1.call-done = bf16[64,2048]{1,0:T(8,128)(2,1)} async-done(((bf16[256,2048]{1,0:T(8,128)(2,1)}), bf16[64,2048]{1,0:T(8,128)(2,1)}) %reduce-scatter.15.cloned.1.call-update) | async-done | bytes 262160 | tf_op jit(solution)/shard_map/reduce_scatter | solution.py:58
  575.5 1.8 select_bitcast_fusion.1
  577.9 1.8 collective-permute-start.1
  579.7 1.1 collective-permute-done.1
  582.3 21.5 %all-gather.18.cloned.1.call-done = bf16[1,256,2048]{2,1,0:T(8,128)(2,1)} async-done(((bf16[1,64,2048]{2,1,0:T(8,128)(2,1)}), bf16[1,256,2048]{2,1,0:T(8,128)(2,1)}) %all-gather.18.cloned.1.call-update) | async-done | bytes 1048592 | tf_op jit(solution)/shard_map/all_gather | solution.py:51
  603.8 17.2 %fusion.33 = bf16[256,8192]{1,0:T(8,128)(2,1)} fusion(bf16[1,8192,2048]{2,1,0:T(8,128)(2,1)} %param.10, bf16[1,256,2048]{2,1,0:T(8,128)(2,1)} %all-gather.18.cloned.1.call-done), kind=kOutput, calls=%fused_computation.50 | convolution fusion | flops 8592031744 | bytes 38797312 | tf_op jit(solution)/shard_map/dot_general | solution.py:50
  621.0 11.0 all-gather.12.cloned.1.call-done
  632.0 16.7 %fusion.30 = bf16[256,8192]{1,0:T(8,128)(2,1)} fusion(bf16[256,2048]{1,0:T(8,128)(2,1)} %all-gather.12.cloned.1.call-done, bf16[1,2048,8192]{2,1,0:T(8,128)(2,1)} %param.9), kind=kOutput, calls=%fused_computation.49 | convolution fusion | flops 8592031744 | bytes 38797312 | tf_op jit(solution)/shard_map/dot_general | solution.py:50
  648.8 291.0 %all-reduce.15.cloned.1.call-done = (bf16[256,8192]{1,0:T(8,128)(2,1)}, bf16[256,8192]{1,0:T(8,128)(2,1)}) async-done(((bf16[256,8192]{1,0:T(8,128)(2,1)}, bf16[256,8192]{1,0:T(8,128)(2,1)}), (bf16[256,8192]{1,0:T(8,128)(2,1)}, bf16[256,8192]{1,0:T(8,128)(2,1)})) %all-reduce.15.cloned.1.call-update) | async-done | bytes 8388624 | tf_op jit(solution)/shard_map/psum | solution.py:56
  939.8 19.9 %fusion.108 = bf16[256,2048]{1,0:T(8,128)(2,1)} fusion(bf16[1,2048,8192]{2,1,0:T(8,128)(2,1)} %param.9, bf16[256,8192]{1,0:T(8,128)(2,1)} %get-tuple-element.5, bf16[256,8192]{1,0:T(8,128)(2,1)} %get-tuple-element.6), kind=kOutput, calls=%fused_computation.113 | convolution fusion | flops 8634499072 | bytes 42991616 | tf_op jit(solution)/shard_map/dot_general | solution.py:59
  959.8 27.0 %reduce-scatter.19.cloned.1.call-done = bf16[64,2048]{1,0:T(8,128)(2,1)} async-done(((bf16[256,2048]{1,0:T(8,128)(2,1)}), bf16[64,2048]{1,0:T(8,128)(2,1)}) %reduce-scatter.19.cloned.1.call-update) | async-done | bytes 262160 | tf_op jit(solution)/shard_map/reduce_scatter | solution.py:58
  987.9 1.3 collective-permute-start.2
  989.2 2.1 collective-permute-done.2
  992.5 26.2 %all-gather.14.cloned.1.call-done = bf16[256,2048]{1,0:T(8,128)(2,1)} async-done(((bf16[64,2048]{1,0:T(8,128)(2,1)}), bf16[256,2048]{1,0:T(8,128)(2,1)}) %all-gather.14.cloned.1.call-update) | async-done | bytes 1048592 | tf_op jit(solution)/shard_map/all_gather | solution.py:51
  1018.7 16.9 %fusion.36 = bf16[256,8192]{1,0:T(8,128)(2,1)} fusion(bf16[256,2048]{1,0:T(8,128)(2,1)} %all-gather.14.cloned.1.call-done, bf16[1,8192,2048]{2,1,0:T(8,128)(2,1)} %param.10), kind=kOutput, calls=%fused_computation.51 | convolution fusion | flops 8592031744 | bytes 38797312 | tf_op jit(solution)/shard_map/dot_general | solution.py:50
  1035.7 155.1 %all-reduce.11.cloned.1.call-done = bf16[256,8192]{1,0:T(8,128)(2,1)} async-done(((bf16[256,8192]{1,0:T(8,128)(2,1)}), bf16[256,8192]{1,0:T(8,128)(2,1)}) %all-reduce.11.cloned.1.call-update) | async-done | bytes 4194320 | tf_op jit(solution)/shard_map/psum | solution.py:56
  1190.8 19.9 %fusion.113 = bf16[256,2048]{1,0:T(8,128)(2,1)} fusion(bf16[1,2048,8192]{2,1,0:T(8,128)(2,1)} %param.9, bf16[256,8192]{1,0:T(8,128)(2,1)} %all-reduce.9.cloned.1.call-done, bf16[256,8192]{1,0:T(8,128)(2,1)} %all-reduce.11.cloned.1.call-done), kind=kOutput, calls=%fused_computation.114 | convolution fusion | flops 8634499072 | bytes 42991616 | tf_op jit(solution)/shard_map/dot_general | solution.py:59
  1210.8 27.0 %reduce-scatter.21.cloned.1.call-done = bf16[64,2048]{1,0:T(8,128)(2,1)} async-done(((bf16[256,2048]{1,0:T(8,128)(2,1)}), bf16[64,2048]{1,0:T(8,128)(2,1)}) %reduce-scatter.21.cloned.1.call-update) | async-done | bytes 262160 | tf_op jit(solution)/shard_map/reduce_scatter | solution.py:58
  1237.8 1.1 select_bitcast_fusion
  1238.9 1.3 collective-permute-start.3
  1240.2 2.1 collective-permute-done.3
  1243.1 26.6 %all-gather.16.cloned.1.call-done = bf16[256,2048]{1,0:T(8,128)(2,1)} async-done(((bf16[64,2048]{1,0:T(8,128)(2,1)}), bf16[256,2048]{1,0:T(8,128)(2,1)}) %all-gather.16.cloned.1.call-update) | async-done | bytes 1048592 | tf_op jit(solution)/shard_map/all_gather | solution.py:51
  1269.7 16.9 %fusion.39 = bf16[256,8192]{1,0:T(8,128)(2,1)} fusion(bf16[256,2048]{1,0:T(8,128)(2,1)} %all-gather.16.cloned.1.call-done, bf16[1,8192,2048]{2,1,0:T(8,128)(2,1)} %param.10), kind=kOutput, calls=%fused_computation.52 | convolution fusion | flops 8592031744 | bytes 38797312 | tf_op jit(solution)/shard_map/dot_general | solution.py:50
  1286.9 19.5 %fusion.133 = bf16[256,2048]{1,0:T(8,128)(2,1)} fusion(bf16[1,8192,2048]{2,1,0:T(8,128)(2,1)} %param.10, bf16[256,8192]{1,0:T(8,128)(2,1)} %get-tuple-element.5), kind=kOutput, calls=%fused_computation.118 | convolution fusion | flops 8611430400 | bytes 38797312 | tf_op jit(solution)/shard_map/dot_general | solution.py:59
  1306.5 135.3 %all-reduce.13.cloned.1.call-done = bf16[256,8192]{1,0:T(8,128)(2,1)} async-done(((bf16[256,8192]{1,0:T(8,128)(2,1)}), bf16[256,8192]{1,0:T(8,128)(2,1)}) %all-reduce.13.cloned.1.call-update) | async-done | bytes 4194320 | tf_op jit(solution)/shard_map/psum | solution.py:56
  1441.8 20.2 %fusion.118 = bf16[256,2048]{1,0:T(8,128)(2,1)} fusion(bf16[1,2048,8192]{2,1,0:T(8,128)(2,1)} %param.9, bf16[256,8192]{1,0:T(8,128)(2,1)} %all-reduce.7.cloned.1.call-done, bf16[256,8192]{1,0:T(8,128)(2,1)} %all-reduce.13.cloned.1.call-done), kind=kOutput, calls=%fused_computation.115 | convolution fusion | flops 8634499072 | bytes 42991616 | tf_op jit(solution)/shard_map/dot_general | solution.py:59
  1462.0 9.5 reduce-scatter.17.cloned.1.call-done
  1471.5 1.1 fusion.141
  1473.4 28.9 %reduce-scatter.23.cloned.1.call-done = bf16[64,2048]{1,0:T(8,128)(2,1)} async-done(((bf16[256,2048]{1,0:T(8,128)(2,1)}), bf16[64,2048]{1,0:T(8,128)(2,1)}) %reduce-scatter.23.cloned.1.call-update) | async-done | bytes 262160 | tf_op jit(solution)/shard_map/reduce_scatter | solution.py:58
  1502.3 1.1 fusion.143
  (73 shorter events, 11.6 us)
Async XLA Ops:
  7.2 44.5 %reduce-scatter.9.cloned.1.call-start = ((), (), s32[]{:S(2)}) async-start(), calls=%async_computation.8 | async-start | bytes 1310720 | tf_op jit(solution)/shard_map/reduce_scatter | solution.py:41
  20.3 60.3 %all-gather.8.cloned.1.call-start = ((), (), s32[]{:S(2)}) async-start(), calls=%async_computation.9 | async-start | bytes 1310720 | tf_op jit(solution)/shard_map/all_gather | solution.py:51
  53.4 199.1 %all-reduce.7.cloned.1.call-start = ((), (), s32[]{:S(2)}) async-start(), calls=%async_computation.10 | async-start | bytes 8388608 | tf_op jit(solution)/shard_map/psum | solution.py:56
  97.4 201.0 %reduce-scatter.11.cloned.1.call-start = ((), (), s32[]{:S(2)}) async-start(), calls=%async_computation.11 | async-start | bytes 1310720 | tf_op jit(solution)/shard_map/reduce_scatter | solution.py:58
  271.2 27.1 %copy-start.8 = (bf16[64,2048]{1,0:T(8,128)(2,1)S(1)}, bf16[64,2048]{1,0:T(8,128)(2,1)}, u32[]{:S(2)}) copy-start(bf16[64,2048]{1,0:T(8,128)(2,1)} %reduce-scatter.9.cloned.1.call-done) | copy-start | bytes 786436
  271.3 57.8 %reduce-scatter.13.cloned.1.call-start = ((), (), s32[]{:S(2)}) async-start(), calls=%async_computation.12 | async-start | bytes 1310720 | tf_op jit(solution)/shard_map/reduce_scatter | solution.py:41
  283.2 74.7 %all-gather.10.cloned.1.call-start = ((), (), s32[]{:S(2)}) async-start(), calls=%async_computation.13 | async-start | bytes 1310720 | tf_op jit(solution)/shard_map/all_gather | solution.py:51
  299.4 29.7 %collective-permute-start = (bf16[64,2048]{1,0:T(8,128)(2,1)S(1)}, bf16[64,2048]{1,0:T(8,128)(2,1)S(1)}, u32[]{:S(2)}, u32[]{:S(2)}) collective-permute-start(bf16[64,2048]{1,0:T(8,128)(2,1)S(1)} %add_convert_fusion.4), channel_id=1, source_target_pairs={{0,16},{1,17},{2,18},{3,19},{4,20},{5,21},{6,22},{7,23},{8,24},{9,... | collective-permute-start | bytes 786440 | tf_op jit(solution)/shard_map/ppermute | solution.py:13
  330.7 198.9 %all-reduce.9.cloned.1.call-start = ((), (), s32[]{:S(2)}) async-start(), calls=%async_computation.14 | async-start | bytes 8388608 | tf_op jit(solution)/shard_map/psum | solution.py:56
  374.5 173.9 %copy-start.2 = (bf16[2,64,2048]{2,1,0:T(8,128)(2,1)S(1)}, bf16[2,64,2048]{2,1,0:T(8,128)(2,1)}, u32[]{:S(2)}) copy-start(bf16[2,64,2048]{2,1,0:T(8,128)(2,1)} %param.11) | copy-start | bytes 1572868
  374.5 201.0 %copy-start = (bf16[64,2048]{1,0:T(8,128)(2,1)S(1)}, bf16[64,2048]{1,0:T(8,128)(2,1)}, u32[]{:S(2)}) copy-start(bf16[64,2048]{1,0:T(8,128)(2,1)} %broadcast_select_fusion.2) | copy-start | bytes 786436
  374.5 200.9 %reduce-scatter.15.cloned.1.call-start = ((), (), s32[]{:S(2)}) async-start(), calls=%async_computation.15 | async-start | bytes 1310720 | tf_op jit(solution)/shard_map/reduce_scatter | solution.py:58
  548.4 55.4 %all-gather.18.cloned.1.call-start = ((), (), s32[]{:S(2)}) async-start(), calls=%async_computation.25 | async-start | bytes 1310720 | tf_op jit(solution)/shard_map/all_gather | solution.py:51
  549.2 82.8 %all-gather.12.cloned.1.call-start = ((), (), s32[]{:S(2)}) async-start(), calls=%async_computation.16 | async-start | bytes 1310720 | tf_op jit(solution)/shard_map/all_gather | solution.py:51
  577.2 0.7 copy-start.4
  577.9 2.9 collective-permute-start.1
  580.8 0.7 copy-start.6
  582.3 357.5 %all-reduce.15.cloned.1.call-start = ((), (), s32[]{:S(2)}) async-start(), calls=%async_computation.26 | async-start | bytes 16777216 | tf_op jit(solution)/shard_map/psum | solution.py:56
  648.8 338.0 %reduce-scatter.19.cloned.1.call-start = ((), (), s32[]{:S(2)}) async-start(), calls=%async_computation.18 | async-start | bytes 1310720 | tf_op jit(solution)/shard_map/reduce_scatter | solution.py:58
  959.7 59.0 %all-gather.14.cloned.1.call-start = ((), (), s32[]{:S(2)}) async-start(), calls=%async_computation.19 | async-start | bytes 1310720 | tf_op jit(solution)/shard_map/all_gather | solution.py:51
  987.9 3.4 collective-permute-start.2
  992.1 198.8 %all-reduce.11.cloned.1.call-start = ((), (), s32[]{:S(2)}) async-start(), calls=%async_computation.20 | async-start | bytes 8388608 | tf_op jit(solution)/shard_map/psum | solution.py:56
  1035.7 202.1 %copy-start.1 = (bf16[64,2048]{1,0:T(8,128)(2,1)S(1)}, bf16[64,2048]{1,0:T(8,128)(2,1)}, u32[]{:S(2)}) copy-start(bf16[64,2048]{1,0:T(8,128)(2,1)} %bitcast_select_fusion) | copy-start | bytes 786436
  1035.7 202.1 %reduce-scatter.21.cloned.1.call-start = ((), (), s32[]{:S(2)}) async-start(), calls=%async_computation.21 | async-start | bytes 1310720 | tf_op jit(solution)/shard_map/reduce_scatter | solution.py:58
  1210.7 59.0 %all-gather.16.cloned.1.call-start = ((), (), s32[]{:S(2)}) async-start(), calls=%async_computation.22 | async-start | bytes 1310720 | tf_op jit(solution)/shard_map/all_gather | solution.py:51
  1238.9 3.4 collective-permute-start.3
  1243.1 198.7 %all-reduce.13.cloned.1.call-start = ((), (), s32[]{:S(2)}) async-start(), calls=%async_computation.23 | async-start | bytes 8388608 | tf_op jit(solution)/shard_map/psum | solution.py:56
  1286.6 184.8 %reduce-scatter.17.cloned.1.call-start = ((), (), s32[]{:S(2)}) async-start(), calls=%async_computation.17 | async-start | bytes 1310720 | tf_op jit(solution)/shard_map/reduce_scatter | solution.py:58
  1306.4 165.1 %copy-start.5 = (bf16[64,2048]{1,0:T(8,128)(2,1)S(1)}, bf16[64,2048]{1,0:T(8,128)(2,1)}, u32[]{:S(2)}) copy-start(bf16[64,2048]{1,0:T(8,128)(2,1)} %copy-done.4) | copy-start | bytes 786436
  1306.4 165.0 %copy-start.7 = (bf16[64,2048]{1,0:T(8,128)(2,1)S(1)}, bf16[64,2048]{1,0:T(8,128)(2,1)}, u32[]{:S(2)}) copy-start(bf16[64,2048]{1,0:T(8,128)(2,1)} %copy-done.6) | copy-start | bytes 786436
  1306.4 166.1 %copy-start.3 = (bf16[1,64,2048]{2,1,0:T(8,128)(2,1)S(1)}, bf16[1,64,2048]{2,1,0:T(8,128)(2,1)}, u32[]{:S(2)}) copy-start(bf16[1,64,2048]{2,1,0:T(8,128)(2,1)} %get-tuple-element.9) | copy-start | bytes 786436
  1306.4 195.9 %reduce-scatter.23.cloned.1.call-start = ((), (), s32[]{:S(2)}) async-start(), calls=%async_computation.24 | async-start | bytes 1310720 | tf_op jit(solution)/shard_map/reduce_scatter | solution.py:58
Sparse Core Ops, SparseCore 0:
  20.4 31.2 reduce-scatter.8
  54.1 26.4 all-gather.7
  97.5 154.9 all-reduce.6
  271.4 26.9 reduce-scatter.10
  301.1 27.9 reduce-scatter.12
  331.3 26.4 all-gather.9
  374.6 154.9 all-reduce.8
  548.5 26.9 reduce-scatter.14
  577.3 26.4 all-gather.17
  605.5 26.4 all-gather.11
  648.9 290.8 all-reduce.14
  959.9 26.9 reduce-scatter.18
  992.2 26.4 all-gather.13
  1035.8 154.9 all-reduce.10
  1210.9 26.9 reduce-scatter.20
  1243.2 26.4 all-gather.15
  1286.8 154.9 all-reduce.12
  1444.5 26.9 reduce-scatter.16
  1474.4 27.9 reduce-scatter.22
where the time goes:
time: 1520 us; the launch traced here: 1510 us
  waiting for transfers between devices  1230 us (81%)
  matrix products  218 us (14%)
  local copies, waits for them, and re-layouts  21.9 us (1%)
  other arithmetic  19.2 us (1%)
    psum x5, waiting for transfers between devices, layer_pass(): lax.psum(partial_sum.astype(jnp.bfloat16), 'mp').astype(jnp.float32)  891 us
    all_gather x6, waiting for transfers between devices, layer_pass(): lax.all_gather(inputs, 'dp', axis=0, tiled=True)  140 us
    reduce_scatter x6, waiting for transfers between devices, layer_pass(): lax.psum_scatter(lax.dot_general(active, second_weight, (((1,), (second_d...  134 us
    dot_general x6, matrix products, layer_pass(): lax.dot_general(active, second_weight, (((1,), (second_dim,)), ((), ())),...  117 us
    dot_general x6, matrix products, layer_pass(): lax.dot_general(lax.all_gather(inputs, 'dp', axis=0, tiled=True), first_w...  101 us
    reduce_scatter x2, waiting for transfers between devices, lookup(): lax.psum_scatter(jnp.where(inside[:, None], fetched.astype(jnp.float32),...  59.4 us
  transfers between devices with their start and end apart: 23, of which 22 were waited for; matrix products, arithmetic and copies ran while one was open for 5% of the time, Pallas kernels for 0%

commit v1 on v0

--- a/solution.py
+++ b/solution.py
@@ -5,6 +5,11 @@
 from jax.sharding import PartitionSpec as P
 
 root_coef = 0.7978845608028654
+
+
+def add_all(x, axis):
+    parts = lax.all_gather(x, axis)
+    return jnp.sum(parts, axis=0)
 
 
 def from_behind(value, axis, steps):
@@ -53,7 +58,7 @@
         (((1,), (first_dim,)), ((), ())),
         preferred_element_type=jnp.float32,
     )
-    summed = lax.psum(partial_sum.astype(jnp.bfloat16), "mp").astype(jnp.float32)
+    summed = add_all(partial_sum.astype(jnp.bfloat16), "mp").astype(jnp.float32)
     active, kept = activate(summed)
     mixed = lax.psum_scatter(
         lax.dot_general(

time: 1520 us -> 2360 us (1.55)
  waiting for transfers between devices: 1230 us -> 1990 us
  other arithmetic: 19.2 us -> 90.7 us
    all_gather x0 -> x6, waiting for transfers between devices: none -> 1670 us  [add_all(): parts = lax.all_gather(x, axis)]
    psum x5 -> x0, waiting for transfers between devices: 891 us -> none  [layer_pass(): lax.psum(partial_sum.astype(jnp.bfloat16), 'mp').astype(jnp.float32)]
    reduce_sum x0 -> x6, other arithmetic: none -> 71.5 us  [add_all(): return jnp.sum(parts, axis=0)]
  transfers between devices with their start and end apart: 23 -> 24, of which waited for: 22 -> 22; matrix products, arithmetic and copies ran while one was open for 5% -> 5% of each run, Pallas kernels for 0% -> 0%
where the time goes in v1:
time: 2360 us; the launch traced here: 2350 us
  waiting for transfers between devices  1990 us (84%)
  matrix products  222 us (9%)
  other arithmetic  90.7 us (4%)
    all_gather x6, waiting for transfers between devices, add_all(): parts = lax.all_gather(x, axis)  1670 us
    all_gather x6, waiting for transfers between devices, layer_pass(): lax.all_gather(inputs, 'dp', axis=0, tiled=True)  139 us
    dot_general x6, matrix products, layer_pass(): lax.dot_general(active, second_weight, (((1,), (second_dim,)), ((), ())),...  119 us
    reduce_scatter x6, waiting for transfers between devices, layer_pass(): lax.psum_scatter(lax.dot_general(active, second_weight, (((1,), (second_d...  118 us
    dot_general x6, matrix products, layer_pass(): lax.dot_general(lax.all_gather(inputs, 'dp', axis=0, tiled=True), first_w...  103 us
    reduce_sum x6, other arithmetic, add_all(): return jnp.sum(parts, axis=0)  71.5 us
    reduce_scatter x2, waiting for transfers between devices, lookup(): lax.psum_scatter(jnp.where(inside[:, None], fetched.astype(jnp.float32),...  59.4 us
  transfers between devices with their start and end apart: 24, of which 22 were waited for; matrix products, arithmetic and copies ran while one was open for 5% of the time, Pallas kernels for 0%

profile of v1, /device:TPU:0, one launch (start us, length us, event | category | flops | bytes accessed | tf_op | source)
XLA Modules:
  0.0 2348.9 jit_solution(14837390863416743052)
XLA Ops:
  8.8 10.1 gather_fusion
  19.0 1.3 select_convert_fusion.1
  20.3 31.3 %reduce-scatter.9.cloned.1.call-done = bf16[64,2048]{1,0:T(8,128)(2,1)} async-done(((bf16[256,2048]{1,0:T(8,128)(2,1)}), bf16[64,2048]{1,0:T(8,128)(2,1)}) %reduce-scatter.9.cloned.1.call-update) | async-done | bytes 262160 | tf_op jit(solution)/shard_map/reduce_scatter | solution.py:46
  51.7 1.7 broadcast_select_fusion.3
  53.4 27.2 %all-gather.20.cloned.1.call-done = bf16[256,2048]{1,0:T(8,128)(2,1)} async-done(((bf16[64,2048]{1,0:T(8,128)(2,1)}), bf16[256,2048]{1,0:T(8,128)(2,1)}) %all-gather.20.cloned.1.call-update) | async-done | bytes 1048592 | tf_op jit(solution)/shard_map/all_gather | solution.py:56
  80.6 16.7 fusion.24
  97.6 286.6 %all-gather.30.cloned.1.call-done = bf16[1024,8192]{1,0:T(8,128)(2,1)} async-done(((bf16[256,8192]{1,0:T(8,128)(2,1)}), bf16[1024,8192]{1,0:T(8,128)(2,1)}) %all-gather.30.cloned.1.call-update) | async-done | bytes 16777232 | tf_op jit(solution)/shard_map/all_gather | solution.py:11
  384.2 11.8 reduce_sum.72
  396.0 18.7 fusion.123
  414.8 10.3 gather_fusion.1
  425.1 1.3 select_convert_fusion
  426.5 14.5 reduce-scatter.11.cloned.1.call-done
  442.1 1.6 collective-permute-start
  443.7 28.1 %reduce-scatter.13.cloned.1.call-done = bf16[64,2048]{1,0:T(8,128)(2,1)} async-done(((bf16[256,2048]{1,0:T(8,128)(2,1)}), bf16[64,2048]{1,0:T(8,128)(2,1)}) %reduce-scatter.13.cloned.1.call-update) | async-done | bytes 262160 | tf_op jit(solution)/shard_map/reduce_scatter | solution.py:46
  471.7 1.7 broadcast_select_fusion.2
  473.7 26.8 %all-gather.22.cloned.1.call-done = bf16[256,2048]{1,0:T(8,128)(2,1)} async-done(((bf16[64,2048]{1,0:T(8,128)(2,1)}), bf16[256,2048]{1,0:T(8,128)(2,1)}) %all-gather.22.cloned.1.call-update) | async-done | bytes 1048592 | tf_op jit(solution)/shard_map/all_gather | solution.py:56
  500.5 16.6 fusion.27
  517.3 286.9 %all-gather.32.cloned.1.call-done = bf16[1024,8192]{1,0:T(8,128)(2,1)} async-done(((bf16[256,8192]{1,0:T(8,128)(2,1)}), bf16[1024,8192]{1,0:T(8,128)(2,1)}) %all-gather.32.cloned.1.call-update) | async-done | bytes 16777232 | tf_op jit(solution)/shard_map/all_gather | solution.py:11
  804.1 11.8 reduce_sum.73
  816.0 18.8 fusion.128
  835.7 25.4 %reduce-scatter.15.cloned.1.call-done = bf16[64,2048]{1,0:T(8,128)(2,1)} async-done(((bf16[256,2048]{1,0:T(8,128)(2,1)}), bf16[64,2048]{1,0:T(8,128)(2,1)}) %reduce-scatter.15.cloned.1.call-update) | async-done | bytes 262160 | tf_op jit(solution)/shard_map/reduce_scatter | solution.py:63
  861.1 1.8 select_bitcast_fusion.1
  863.6 1.6 collective-permute-start.1
  868.2 21.2 all-gather.36.cloned.1.call-done
  889.5 17.2 fusion.33
  906.7 11.0 all-gather.24.cloned.1.call-done
  917.7 19.0 fusion.30
  936.9 269.2 %all-gather.38.cloned.1.call-done = bf16[1024,8192]{1,0:T(8,128)(2,1)} async-done(((bf16[256,8192]{1,0:T(8,128)(2,1)}), bf16[1024,8192]{1,0:T(8,128)(2,1)}) %all-gather.38.cloned.1.call-update) | async-done | bytes 16777232 | tf_op jit(solution)/shard_map/all_gather | solution.py:11
  1206.0 12.5 reduce_sum.75
  1218.5 273.9 %all-gather.34.cloned.1.call-done = bf16[1024,8192]{1,0:T(8,128)(2,1)} async-done(((bf16[256,8192]{1,0:T(8,128)(2,1)}), bf16[1024,8192]{1,0:T(8,128)(2,1)}) %all-gather.34.cloned.1.call-update) | async-done | bytes 16777232 | tf_op jit(solution)/shard_map/all_gather | solution.py:11
  1492.4 11.8 reduce_sum.74
  1504.3 19.9 fusion.108
  1524.3 26.2 %reduce-scatter.19.cloned.1.call-done = bf16[64,2048]{1,0:T(8,128)(2,1)} async-done(((bf16[256,2048]{1,0:T(8,128)(2,1)}), bf16[64,2048]{1,0:T(8,128)(2,1)}) %reduce-scatter.19.cloned.1.call-update) | async-done | bytes 262160 | tf_op jit(solution)/shard_map/reduce_scatter | solution.py:63
  1552.8 2.1 collective-permute-done.2
  1555.7 26.6 %all-gather.26.cloned.1.call-done = bf16[256,2048]{1,0:T(8,128)(2,1)} async-done(((bf16[64,2048]{1,0:T(8,128)(2,1)}), bf16[256,2048]{1,0:T(8,128)(2,1)}) %all-gather.26.cloned.1.call-update) | async-done | bytes 1048592 | tf_op jit(solution)/shard_map/all_gather | solution.py:56
  1582.4 16.9 fusion.36
  1599.5 286.7 %all-gather.40.cloned.1.call-done = bf16[1024,8192]{1,0:T(8,128)(2,1)} async-done(((bf16[256,8192]{1,0:T(8,128)(2,1)}), bf16[1024,8192]{1,0:T(8,128)(2,1)}) %all-gather.40.cloned.1.call-update) | async-done | bytes 16777232 | tf_op jit(solution)/shard_map/all_gather | solution.py:11
  1886.2 11.7 reduce_sum.76
  1897.9 20.0 fusion.113
  1918.0 26.2 %reduce-scatter.21.cloned.1.call-done = bf16[64,2048]{1,0:T(8,128)(2,1)} async-done(((bf16[256,2048]{1,0:T(8,128)(2,1)}), bf16[64,2048]{1,0:T(8,128)(2,1)}) %reduce-scatter.21.cloned.1.call-update) | async-done | bytes 262160 | tf_op jit(solution)/shard_map/reduce_scatter | solution.py:63
  1946.6 2.1 collective-permute-done.3
  1949.5 26.6 %all-gather.28.cloned.1.call-done = bf16[256,2048]{1,0:T(8,128)(2,1)} async-done(((bf16[64,2048]{1,0:T(8,128)(2,1)}), bf16[256,2048]{1,0:T(8,128)(2,1)}) %all-gather.28.cloned.1.call-update) | async-done | bytes 1048592 | tf_op jit(solution)/shard_map/all_gather | solution.py:56
  1976.1 16.9 fusion.39
  1993.3 21.1 fusion.133
  2014.5 265.5 %all-gather.42.cloned.1.call-done = bf16[1024,8192]{1,0:T(8,128)(2,1)} async-done(((bf16[256,8192]{1,0:T(8,128)(2,1)}), bf16[1024,8192]{1,0:T(8,128)(2,1)}) %all-gather.42.cloned.1.call-update) | async-done | bytes 16777232 | tf_op jit(solution)/shard_map/all_gather | solution.py:11
  2279.9 11.9 reduce_sum.77
  2291.8 20.4 fusion.118
  2314.2 25.4 %reduce-scatter.23.cloned.1.call-done = bf16[64,2048]{1,0:T(8,128)(2,1)} async-done(((bf16[256,2048]{1,0:T(8,128)(2,1)}), bf16[64,2048]{1,0:T(8,128)(2,1)}) %reduce-scatter.23.cloned.1.call-update) | async-done | bytes 262160 | tf_op jit(solution)/shard_map/reduce_scatter | solution.py:63
  (82 shorter events, 19.3 us)
Async XLA Ops:
  7.2 44.5 %reduce-scatter.9.cloned.1.call-start = ((), (), s32[]{:S(2)}) async-start(), calls=%async_computation.8 | async-start | bytes 1310720 | tf_op jit(solution)/shard_map/reduce_scatter | solution.py:46
  20.3 60.3 %all-gather.20.cloned.1.call-start = ((), (), s32[]{:S(2)}) async-start(), calls=%async_computation.9 | async-start | bytes 1310720 | tf_op jit(solution)/shard_map/all_gather | solution.py:56
  53.4 330.9 %all-gather.30.cloned.1.call-start = ((), (), s32[]{:S(2)}) async-start(), calls=%async_computation.21 | async-start | bytes 20971520 | tf_op jit(solution)/shard_map/all_gather | solution.py:11
  97.3 343.7 %reduce-scatter.11.cloned.1.call-start = ((), (), s32[]{:S(2)}) async-start(), calls=%async_computation.10 | async-start | bytes 1310720 | tf_op jit(solution)/shard_map/reduce_scatter | solution.py:63
  414.7 26.3 %copy-start.8 = (bf16[64,2048]{1,0:T(8,128)(2,1)S(1)}, bf16[64,2048]{1,0:T(8,128)(2,1)}, u32[]{:S(2)}) copy-start(bf16[64,2048]{1,0:T(8,128)(2,1)} %reduce-scatter.9.cloned.1.call-done) | copy-start | bytes 786436
  414.7 57.0 %reduce-scatter.13.cloned.1.call-start = ((), (), s32[]{:S(2)}) async-start(), calls=%async_computation.11 | async-start | bytes 1310720 | tf_op jit(solution)/shard_map/reduce_scatter | solution.py:46
  426.5 74.1 %all-gather.22.cloned.1.call-start = ((), (), s32[]{:S(2)}) async-start(), calls=%async_computation.12 | async-start | bytes 1310720 | tf_op jit(solution)/shard_map/all_gather | solution.py:56
  442.1 29.7 %collective-permute-start = (bf16[64,2048]{1,0:T(8,128)(2,1)S(1)}, bf16[64,2048]{1,0:T(8,128)(2,1)S(1)}, u32[]{:S(2)}, u32[]{:S(2)}) collective-permute-start(bf16[64,2048]{1,0:T(8,128)(2,1)S(1)} %add_convert_fusion.4), channel_id=1, source_target_pairs={{0,16},{1,17},{2,18},{3,19},{4,20},{5,21},{6,22},{7,23},{8,24},{9,... | collective-permute-start | bytes 786440 | tf_op jit(solution)/shard_map/ppermute | solution.py:18
  473.4 330.7 %all-gather.32.cloned.1.call-start = ((), (), s32[]{:S(2)}) async-start(), calls=%async_computation.22 | async-start | bytes 20971520 | tf_op jit(solution)/shard_map/all_gather | solution.py:11
  517.2 343.9 %reduce-scatter.15.cloned.1.call-start = ((), (), s32[]{:S(2)}) async-start(), calls=%async_computation.13 | async-start | bytes 1310720 | tf_op jit(solution)/shard_map/reduce_scatter | solution.py:63
  815.9 18.9 copy-start.2
  815.9 45.1 %copy-start = (bf16[64,2048]{1,0:T(8,128)(2,1)S(1)}, bf16[64,2048]{1,0:T(8,128)(2,1)}, u32[]{:S(2)}) copy-start(bf16[64,2048]{1,0:T(8,128)(2,1)} %broadcast_select_fusion.2) | copy-start | bytes 786436
  834.8 54.7 %all-gather.36.cloned.1.call-start = ((), (), s32[]{:S(2)}) async-start(), calls=%async_computation.24 | async-start | bytes 1310720 | tf_op jit(solution)/shard_map/all_gather | solution.py:56
  835.6 82.1 %all-gather.24.cloned.1.call-start = ((), (), s32[]{:S(2)}) async-start(), calls=%async_computation.14 | async-start | bytes 1310720 | tf_op jit(solution)/shard_map/all_gather | solution.py:56
  862.9 0.7 copy-start.4
  863.6 2.7 collective-permute-start.1
  866.3 0.7 copy-start.6
  867.7 338.3 %all-gather.38.cloned.1.call-start = ((), (), s32[]{:S(2)}) async-start(), calls=%async_computation.25 | async-start | bytes 20971520 | tf_op jit(solution)/shard_map/all_gather | solution.py:11
  906.6 585.8 %all-gather.34.cloned.1.call-start = ((), (), s32[]{:S(2)}) async-start(), calls=%async_computation.23 | async-start | bytes 20971520 | tf_op jit(solution)/shard_map/all_gather | solution.py:11
  936.7 613.8 %reduce-scatter.19.cloned.1.call-start = ((), (), s32[]{:S(2)}) async-start(), calls=%async_computation.16 | async-start | bytes 1310720 | tf_op jit(solution)/shard_map/reduce_scatter | solution.py:63
  1524.2 58.2 %all-gather.26.cloned.1.call-start = ((), (), s32[]{:S(2)}) async-start(), calls=%async_computation.17 | async-start | bytes 1310720 | tf_op jit(solution)/shard_map/all_gather | solution.py:56
  1551.5 3.4 collective-permute-start.2
  1555.7 330.5 %all-gather.40.cloned.1.call-start = ((), (), s32[]{:S(2)}) async-start(), calls=%async_computation.26 | async-start | bytes 20971520 | tf_op jit(solution)/shard_map/all_gather | solution.py:11
  1599.2 344.9 %reduce-scatter.21.cloned.1.call-start = ((), (), s32[]{:S(2)}) async-start(), calls=%async_computation.18 | async-start | bytes 1310720 | tf_op jit(solution)/shard_map/reduce_scatter | solution.py:63
  1897.9 46.3 %copy-start.1 = (bf16[64,2048]{1,0:T(8,128)(2,1)S(1)}, bf16[64,2048]{1,0:T(8,128)(2,1)}, u32[]{:S(2)}) copy-start(bf16[64,2048]{1,0:T(8,128)(2,1)} %bitcast_select_fusion) | copy-start | bytes 786436
  1917.9 58.2 %all-gather.28.cloned.1.call-start = ((), (), s32[]{:S(2)}) async-start(), calls=%async_computation.19 | async-start | bytes 1310720 | tf_op jit(solution)/shard_map/all_gather | solution.py:56
  1945.3 3.4 collective-permute-start.3
  1949.5 330.5 %all-gather.42.cloned.1.call-start = ((), (), s32[]{:S(2)}) async-start(), calls=%async_computation.27 | async-start | bytes 20971520 | tf_op jit(solution)/shard_map/all_gather | solution.py:11
  1993.0 319.3 %reduce-scatter.17.cloned.1.call-start = ((), (), s32[]{:S(2)}) async-start(), calls=%async_computation.15 | async-start | bytes 1310720 | tf_op jit(solution)/shard_map/reduce_scatter | solution.py:63
  2014.4 325.3 %reduce-scatter.23.cloned.1.call-start = ((), (), s32[]{:S(2)}) async-start(), calls=%async_computation.20 | async-start | bytes 1310720 | tf_op jit(solution)/shard_map/reduce_scatter | solution.py:63
  2291.8 20.5 copy-start.5
  2291.8 20.5 copy-start.7
  2291.8 21.6 copy-start.3
Sparse Core Ops, SparseCore 0:
  20.4 31.2 reduce-scatter.8
  54.1 26.4 all-gather.19
  97.4 286.7 all-gather.29
  414.9 26.0 reduce-scatter.10
  443.8 27.9 reduce-scatter.12
  474.0 26.4 all-gather.21
  517.3 286.7 all-gather.31
  834.9 26.1 reduce-scatter.14
  862.9 26.4 all-gather.35
  891.2 26.4 all-gather.23
  919.3 286.7 all-gather.37
  1207.5 284.9 all-gather.33
  1524.3 26.0 reduce-scatter.18
  1555.8 26.5 all-gather.25
  1599.4 286.7 all-gather.39
  1918.0 26.1 reduce-scatter.20
  1949.6 26.4 all-gather.27
  1993.1 286.7 all-gather.41
  2282.8 26.0 reduce-scatter.16
  2312.4 27.2 reduce-scatter.22
